TPU v7x, 256 devices: a whole 4x4x8 slice. The times are simulated.
256 devices in a mesh: view: 4 (over y_lo, core), ctx: 64 (over x, y_hi, z).
Axes of the slice: x: 4, y: 4 (y_hi: 2, y_lo: 2; y = y_hi * 2 + y_lo), z: 8, core: 2. Of those that a mesh axis runs over, the one named last changes fastest.
Arguments:
- q_self: bfloat16 [4, 7168, 1024], P('view', 'ctx'), may hold values from -16 to 16
- k_self: bfloat16 [4, 7168, 1024], P('view', 'ctx'), may hold values from -16 to 16
- v_self: bfloat16 [4, 7168, 1024], P('view', 'ctx'), may hold values from -6 to 6
- q_cross: bfloat16 [4, 7168, 1024], P('view', 'ctx'), may hold values from -16 to 16
- k_cross: bfloat16 [4, 7168, 1024], P('view', 'ctx'), may hold values from -16 to 16
- v_cross: bfloat16 [4, 7168, 1024], P('view', 'ctx'), may hold values from -6 to 6
Outputs:
- block_out: bfloat16 [4, 7168, 1024], P('view', 'ctx')
All inputs are finite; a program needn't handle non-finite values.
Results may differ from a plain program's by a relative error of at most 0.01.
Values may be sent and summed in bfloat16 or wider, within the bound.
A program may use at most 128 MiB of HBM per device.

v0:
```python
import math

import jax
import jax.numpy as jnp
from jax import lax
from jax.sharding import PartitionSpec as P

HEAD = 128


def cross_attend(pieces):
    cross_query, key_four, value_four = pieces
    score_scale = 1.0 / math.sqrt(HEAD)
    cross_scores = (
        jnp.einsum("atnd,btnd->tnab", cross_query, key_four, preferred_element_type=jnp.float32)
        * score_scale
    )
    cross_scores = cross_scores - jnp.max(cross_scores, axis=-1, keepdims=True)
    weights_full = jnp.exp(cross_scores)
    cross_weights = (weights_full / jnp.sum(weights_full, axis=-1, keepdims=True)).astype(
        jnp.bfloat16
    )
    return jnp.einsum(
        "tnab,btnd->atnd", cross_weights, value_four, preferred_element_type=jnp.float32
    ).astype(jnp.bfloat16)


def start_state(view_count, head_count, row_count):
    return (
        jnp.full((view_count, head_count, row_count), -1e30, jnp.float32),
        jnp.zeros((view_count, head_count, row_count), jnp.float32),
        jnp.zeros((view_count, head_count, row_count, HEAD), jnp.float32),
    )


def online_update(queries, state_now, key_rows, value_rows):
    score_scale = 1.0 / math.sqrt(HEAD)
    running_max, running_sum, weighted = state_now
    scores = (
        jnp.einsum("aqhd,akhd->ahqk", queries, key_rows, preferred_element_type=jnp.float32)
        * score_scale
    )
    new_max = jnp.maximum(running_max, jnp.max(scores, axis=-1))
    weights_full = jnp.exp(scores - new_max[..., None])
    running_sum = jnp.sum(weights_full, axis=-1)
    update = jnp.einsum(
        "ahqk,akhd->ahqd",
        weights_full.astype(jnp.bfloat16),
        value_rows,
        preferred_element_type=jnp.float32,
    )
    weighted = update
    return (new_max, running_sum, weighted)


def finish_state(state_now):
    attended = state_now[2] / state_now[1][..., None]
    return jnp.transpose(attended, (0, 2, 1, 3)).astype(jnp.bfloat16)


def body(q_self, k_self, v_self, q_cross, k_cross, v_cross):
    view_count, row_count, feature_width = q_self.shape
    head_count = feature_width // HEAD
    queries = q_self.reshape(view_count, row_count, head_count, HEAD)
    initial = start_state(view_count, head_count, row_count)
    key_rows = lax.all_gather(k_self, "ctx", axis=1, tiled=True).reshape(
        view_count, -1, head_count, HEAD
    )
    value_rows = lax.all_gather(v_self, "ctx", axis=1, tiled=True).reshape(
        view_count, -1, head_count, HEAD
    )
    final_state = online_update(queries, initial, key_rows, value_rows)
    o_self = finish_state(final_state)
    merged = (
        q_cross.reshape(view_count, row_count, head_count, HEAD).astype(jnp.float32)
        + o_self.astype(jnp.float32)
    ).astype(jnp.bfloat16)
    key_four = k_cross.reshape(view_count, row_count, head_count, HEAD)
    value_four = v_cross.reshape(view_count, row_count, head_count, HEAD)
    mixed_out = cross_attend(
        (
            lax.all_to_all(merged, "view", split_axis=1, concat_axis=0, tiled=True),
            lax.all_to_all(key_four, "view", split_axis=1, concat_axis=0, tiled=True),
            lax.all_to_all(value_four, "view", split_axis=1, concat_axis=0, tiled=True),
        )
    )
    o_cross = lax.all_to_all(mixed_out, "view", split_axis=0, concat_axis=1, tiled=True)
    total_out = o_self.astype(jnp.float32) + o_cross.astype(jnp.float32)
    return total_out.reshape(view_count, row_count, feature_width).astype(jnp.bfloat16)


def solution(mesh):
    in_specs = (
        P("view", "ctx", None),
        P("view", "ctx", None),
        P("view", "ctx", None),
        P("view", "ctx", None),
        P("view", "ctx", None),
        P("view", "ctx", None),
    )
    out_specs = P("view", "ctx", None)
    return jax.shard_map(body, mesh=mesh, in_specs=in_specs, out_specs=out_specs, check_vma=False)
```

profile of v0, /device:TPU:1, one launch (start us, length us, event | category | flops | bytes accessed | tf_op | source)
XLA Modules:
  0.0 455.5 jit_solution(1096666454138404234)
XLA Ops:
  6.5 0.0 all-gather.3.cloned.1.call-start
  6.5 0.7 all-gather.3.cloned.1.call-update
  7.3 0.0 all-gather.5.cloned.1.call-start
  7.3 0.7 all-gather.5.cloned.1.call-update
  8.0 1.7 copy.45
  9.7 6.6 %all-to-all-start.1 = ((bf16[1,112,8,128]{3,2,0,1:T(8,128)(2,1)}), bf16[1,112,8,128]{3,2,0,1:T(8,128)(2,1)S(1)}, u32[]{:S(2)}, u32[]{:S(2)}) async-start(bf16[1,112,8,128]{3,2,0,1:T(8,128)(2,1)} %bitcast.25), calls=%async_computation.1 | async-start | bytes 458752 | tf_op jit(solution)/shard_map/all_to_all | solution.py:83
  16.2 1.0 copy.43
  17.2 1.0 convert_bitcast_fusion
  18.2 0.1 copy.44
  18.3 180.3 %all-gather.3.cloned.1.call-done = bf16[1,7168,1024]{2,1,0:T(8,128)(2,1)} async-done(((bf16[1,112,1024]{2,1,0:T(8,128)(2,1)}), bf16[1,7168,1024]{2,1,0:T(8,128)(2,1)}) %all-gather.3.cloned.1.call-update) | async-done | bytes 14680080 | tf_op jit(solution)/shard_map/all_gather | solution.py:66
  198.6 18.4 %copy.25 = bf16[1,7168,1024]{1,2,0:T(8,128)(2,1)} copy(bf16[1,7168,1024]{2,1,0:T(8,128)(2,1)} %all-gather.3.cloned.1.call-done) | data formatting | bytes 29360128 | tf_op jit(solution)/shard_map/all_gather | solution.py:66
  217.0 13.5 %multiply_reduce_fusion = (f32[8,112]{1,0:T(8,128)S(1)}, f32[8,112,7168]{2,1,0:T(8,128)}) fusion(bf16[7168,8,128]{0,2,1:T(8,128)(2,1)} %bitcast.47, bf16[112,8,128]{2,1,0:T(8,128)(2,1)S(1)} %bitcast.49), kind=kOutput, calls=%fused_computation.2 | convolution fusion | flops 1657011328 | bytes 40603136 | tf_op jit(solution)/shard_map/aqhd,akhd->ahqk/dot_general | solution.py:40
  230.5 11.0 %fusion.1 = f32[8,112]{1,0:T(8,128)S(1)} fusion(f32[8,112,7168]{2,1,0:T(8,128)} %get-tuple-element.6, f32[8,112]{1,0:T(8,128)S(1)} %broadcast_maximum_fusion), kind=kLoop, calls=%fused_computation.3 | loop fusion | flops 19266688 | bytes 25697280 | tf_op jit(solution)/shard_map/reduce_sum | solution.py:45
  241.6 142.0 %all-gather.5.cloned.1.call-done = bf16[1,7168,1024]{2,1,0:T(8,128)(2,1)} async-done(((bf16[1,112,1024]{2,1,0:T(8,128)(2,1)}), bf16[1,7168,1024]{2,1,0:T(8,128)(2,1)}) %all-gather.5.cloned.1.call-update) | async-done | bytes 14680080 | tf_op jit(solution)/shard_map/all_gather | solution.py:69
  383.6 18.4 %copy.28 = bf16[1,7168,1024]{1,2,0:T(8,128)(2,1)} copy(bf16[1,7168,1024]{2,1,0:T(8,128)(2,1)} %all-gather.5.cloned.1.call-done) | data formatting | bytes 29360128 | tf_op jit(solution)/shard_map/all_gather | solution.py:69
  402.0 0.0 copy-start
  402.0 18.1 %fusion.26 = (bf16[1,112,8,128]{3,1,2,0:T(8,128)(2,1)S(1)}, f32[1,112,8,128]{3,1,2,0:T(8,128)S(1)}) fusion(f32[1,112,8,128]{3,2,0,1:T(8,128)S(1)} %bitcast.48, f32[8,112]{1,0:T(8,128)S(1)} %fusion.1, bf16[7168,8,128]{0,2,1:T(8,128)(2,1)} %bitcast.46, f32[8,112,7168]{2,1,0:T(8,128)} %get-tuple-element.6, f32[8,112]{1,0:T(8,128)S(1)} %broadcast_maximum_fusion), kind=kOutput, calls=%fused_computation.21 | convolution fusion | flops 1664008192 | bytes 41524224 | tf_op jit(solution)/shard_map/ahqk,akhd->ahqd/dot_general | solution.py:46
  420.1 0.7 copy.31
  420.8 0.0 all-to-all-done.1
  420.8 4.8 %all-to-all-start = ((bf16[1,112,8,128]{3,2,0,1:T(8,128)(2,1)}), bf16[1,112,8,128]{3,2,0,1:T(8,128)(2,1)S(1)}, u32[]{:S(2)}, u32[]{:S(2)}) async-start(bf16[1,112,8,128]{3,2,0,1:T(8,128)(2,1)} %copy.31), calls=%async_computation | async-start | bytes 458752 | tf_op jit(solution)/shard_map/all_to_all | solution.py:82
  425.6 0.0 copy-done
  425.6 0.7 copy.46
  426.3 4.0 all-to-all-done
  430.3 4.3 all-to-all-start.2
  434.6 0.8 fusion.45
  435.4 3.9 all-to-all-done.2
  439.3 0.5 fusion.9
  439.8 8.1 %all_to_all.45 = bf16[4,28,8,128]{3,2,1,0:T(8,128)(2,1)S(1)} all-to-all(bf16[4,28,8,128]{3,2,1,0:T(8,128)(2,1)S(1)} %copy.36), channel_id=1, replica_groups=mesh['view'=4,'ctx'=64] {'view'}, dimensions={0} | all-to-all | bytes 458752 | tf_op jit(solution)/shard_map/all_to_all | solution.py:87
  447.9 0.8 copy_bitcast_fusion
  (3 shorter events, 0.1 us)
Async XLA Ops:
  6.5 192.1 %all-gather.3.cloned.1.call-start = ((), (), s32[]{:S(2)}) async-start(), calls=%async_computation.4 | async-start | bytes 14909440 | tf_op jit(solution)/shard_map/all_gather | solution.py:66
  7.3 376.3 %all-gather.5.cloned.1.call-start = ((), (), s32[]{:S(2)}) async-start(), calls=%async_computation.5 | async-start | bytes 14909440 | tf_op jit(solution)/shard_map/all_gather | solution.py:69
  9.7 411.2 %all-to-all-start.1 = ((bf16[1,112,8,128]{3,2,0,1:T(8,128)(2,1)}), bf16[1,112,8,128]{3,2,0,1:T(8,128)(2,1)S(1)}, u32[]{:S(2)}, u32[]{:S(2)}) async-start(bf16[1,112,8,128]{3,2,0,1:T(8,128)(2,1)} %bitcast.25), calls=%async_computation.1 | async-start | bytes 458752 | tf_op jit(solution)/shard_map/all_to_all | solution.py:83
  402.0 23.6 %copy-start = (bf16[1,112,1024]{2,1,0:T(8,128)(2,1)S(1)}, bf16[1,112,1024]{2,1,0:T(8,128)(2,1)}, u32[]{:S(2)}) copy-start(bf16[1,112,1024]{2,1,0:T(8,128)(2,1)} %param.11) | copy-start | bytes 688132
  420.8 9.4 %all-to-all-start = ((bf16[1,112,8,128]{3,2,0,1:T(8,128)(2,1)}), bf16[1,112,8,128]{3,2,0,1:T(8,128)(2,1)S(1)}, u32[]{:S(2)}, u32[]{:S(2)}) async-start(bf16[1,112,8,128]{3,2,0,1:T(8,128)(2,1)} %copy.31), calls=%async_computation | async-start | bytes 458752 | tf_op jit(solution)/shard_map/all_to_all | solution.py:82
  430.3 9.0 %all-to-all-start.2 = ((bf16[1,112,8,128]{3,2,0,1:T(8,128)(2,1)}), bf16[1,112,8,128]{3,2,0,1:T(8,128)(2,1)S(1)}, u32[]{:S(2)}, u32[]{:S(2)}) async-start(bf16[1,112,8,128]{3,2,0,1:T(8,128)(2,1)} %bitcast.30), calls=%async_computation.2 | async-start | bytes 458752 | tf_op jit(solution)/shard_map/all_to_all | solution.py:84
Sparse Core Ops, SparseCore 0:
  10.9 187.6 all-gather.2
  202.2 181.3 all-gather.4
where the time goes:
time: 457 us; the launch traced here: 456 us
  waiting for transfers between devices  332 us (73%)
  local copies, waits for them, and re-layouts  41.1 us (9%)
  matrix products  32.9 us (7%)
  starting transfers between devices  15.7 us (3%)
  between operations  13.5 us (3%)
  other arithmetic  12.8 us (3%)
  blocking collectives  8.08 us (2%)
    all_gather x1, waiting for transfers between devices, body(): lax.all_gather(k_self, 'ctx', axis=1, tiled=True)  180 us
    all_gather x1, waiting for transfers between devices, body(): lax.all_gather(v_self, 'ctx', axis=1, tiled=True)  142 us
    all_gather x1, local copies, waits for them, and re-layouts, body(): lax.all_gather(k_self, 'ctx', axis=1, tiled=True)  18.4 us
    all_gather x1, local copies, waits for them, and re-layouts, body(): lax.all_gather(v_self, 'ctx', axis=1, tiled=True)  18.4 us
    dot_general x1, matrix products, online_update(): jnp.einsum('ahqk,akhd->ahqd', weights_full.astype(jnp.bfloat16), value_ro...  18.1 us
    dot_general x1, matrix products, online_update(): jnp.einsum('aqhd,akhd->ahqk', queries, key_rows, preferred_element_type=j...  13.5 us
    reduce_sum x1, other arithmetic, online_update(): running_sum = jnp.sum(weights_full, axis=-1)  11 us
  transfers between devices with their start and end apart: 5, of which 4 were waited for; matrix products, arithmetic and copies ran while one was open for 19% of the time, Pallas kernels for 0%

commit v1 on v0

v1 whole, which is shorter than its diff:
```python
import functools
import math

import jax
import jax.numpy as jnp
from jax import lax
from jax.experimental import pallas as pl
from jax.experimental.pallas import tpu as pltpu
from jax.sharding import PartitionSpec as P

HEAD = 128
HEADS = 8
ROWS = 112
BLOCK = HEADS * ROWS
TILE = 128
SCALE = 1.0 / math.sqrt(HEAD)
SCALE2 = SCALE * math.log2(math.e)
MESH = pl.DeviceIdType.MESH
NT = (((1,), (1,)), ((), ()))


def kernel(
    q_in, k_in, v_in, qc_in, kc_in, vc_in, out_ref,
    qbuf, kbuf, vbuf, kcb, vcb, qcb, obuf, ohome, acc, mrow, lrow,
    send_a, recv_a, send_x, recv_x, send_p, recv_p, send_c, recv_c, send_o, recv_o, loc,
):
    view = lax.axis_index("view")
    ctx = lax.axis_index("ctx")
    ylo, core = view // 2, view % 2
    x, yhi, z = ctx // 16, (ctx // 8) % 2, ctx % 8
    rest = ctx % 16
    right = ((x + 1) % 4) * 16 + rest
    left = ((x + 3) % 4) * 16 + rest
    partner = ylo * 2 + (1 - core)
    other = (1 - ylo) * 2 + core
    peer_view = ylo * 2 + yhi
    peer_ctx = x * 16 + core * 8
    same = core == yhi

    barrier = pltpu.get_barrier_semaphore()
    for dev in ((view, right), (view, left), (partner, ctx), (other, ctx)):
        pl.semaphore_signal(barrier, inc=1, device_id=dev, device_id_type=MESH)
    for d in range(1, 8):
        pl.semaphore_signal(
            barrier, inc=1, device_id=(peer_view, peer_ctx + (z + d) % 8), device_id_type=MESH
        )

    @pl.when(jnp.logical_not(same))
    def _():
        pl.semaphore_signal(barrier, inc=1, device_id=(peer_view, peer_ctx + z), device_id_type=MESH)

    pl.semaphore_wait(barrier, 11 + (core + yhi) % 2)

    my_rows = pl.ds(pl.multiple_of(z * ROWS, 16), ROWS)

    def spread(n, src, dst):
        for d in range(8):
            h = (z + d) % 8
            piece = src.at[:, pl.ds(pl.multiple_of(h * HEAD, HEAD), HEAD)]

            def remote():
                pltpu.make_async_remote_copy(
                    src_ref=piece, dst_ref=dst, send_sem=send_a.at[n, d], recv_sem=recv_a.at[n],
                    device_id=(peer_view, peer_ctx + h), device_id_type=MESH,
                ).start()

            if d:
                remote()
            else:
                pl.when(jnp.logical_not(same))(remote)

                @pl.when(same)
                def _():
                    pltpu.make_async_copy(piece, dst, recv_a.at[n]).start()

    spread(0, k_in, kbuf.at[0, my_rows, :])
    spread(1, v_in, vbuf.at[0, my_rows, :])
    spread(2, q_in, qbuf.at[my_rows, :])

    def push(src, dst, send, recv, dev):
        copy = pltpu.make_async_remote_copy(
            src_ref=src, dst_ref=dst, send_sem=send, recv_sem=recv, device_id=dev, device_id_type=MESH
        )
        copy.start()
        return copy

    sent = []
    for n, (src, buf) in enumerate(((kc_in, kcb), (vc_in, vcb))):
        sent.append(push(src, buf.at[2], send_c.at[n, 0], recv_c.at[n, 0], (other, ctx)))
        sent.append(push(src, buf.at[1], send_c.at[n, 1], recv_c.at[n, 1], (partner, ctx)))
    own = [
        pltpu.make_async_copy(kc_in, kcb.at[0], loc.at[0]),
        pltpu.make_async_copy(vc_in, vcb.at[0], loc.at[1]),
        pltpu.make_async_copy(qc_in, qcb, loc.at[2]),
    ]
    for copy in own:
        copy.start()

    bufs = (kbuf, vbuf)
    half = BLOCK // 2

    def got(buf, sem):
        pltpu.make_async_copy(buf, buf, sem).wait()

    def share(n, slot):
        sent.append(
            push(bufs[n].at[slot], bufs[n].at[4 + slot], send_p.at[n, slot], recv_p.at[n, slot], (partner, ctx))
        )

    for n in range(2):
        got(bufs[n].at[0], recv_a.at[n])
        sent.append(push(bufs[n].at[0], bufs[n].at[1], send_x.at[n, 0], recv_x.at[n, 0], (view, right)))
        sent.append(push(bufs[n].at[0], bufs[n].at[2], send_x.at[n, 1], recv_x.at[n, 1], (view, left)))
        share(n, 0)

    def relay(n):
        buf = bufs[n]
        got(buf.at[1], recv_x.at[n, 0])
        low = buf.at[1, pl.ds(0, half), :]
        sent.append(push(low, buf.at[3, pl.ds(0, half), :], send_x.at[n, 2], recv_x.at[n, 2], (view, right)))
        share(n, 1)
        got(buf.at[2], recv_x.at[n, 1])
        high = buf.at[2, pl.ds(half, half), :]
        sent.append(push(high, buf.at[3, pl.ds(half, half), :], send_x.at[n, 3], recv_x.at[n, 3], (view, left)))
        share(n, 2)

    def last(n):
        buf = bufs[n]
        got(buf.at[3, pl.ds(0, half), :], recv_x.at[n, 2])
        got(buf.at[3, pl.ds(half, half), :], recv_x.at[n, 3])
        share(n, 3)

    def attend(slot, first=False):
        def step(t, carry):
            rows = pl.ds(pl.multiple_of(t * TILE, TILE), TILE)
            scores = lax.dot_general(
                qbuf[rows, :], kbuf[slot], NT, preferred_element_type=jnp.float32
            )
            top = jnp.max(scores, axis=1, keepdims=True)
            if not first:
                old = mrow[rows, :]
                top = jnp.maximum(old, top)
            weights = jnp.exp2((scores - top) * SCALE2)
            total = jnp.sum(weights, axis=1, keepdims=True)
            update = jnp.dot(
                weights.astype(jnp.bfloat16), vbuf[slot], preferred_element_type=jnp.float32
            )
            if not first:
                fade = jnp.exp2((old - top) * SCALE2)
                total = total + fade * lrow[rows, :]
                update = update + fade * acc[rows, :]
            mrow[rows, :] = top
            lrow[rows, :] = total
            acc[rows, :] = update
            return carry

        lax.fori_loop(0, BLOCK // TILE, step, 0)

    got(qbuf, recv_a.at[2])
    attend(0, first=True)
    relay(0)
    got(kbuf.at[4], recv_p.at[0, 0])
    got(vbuf.at[4], recv_p.at[1, 0])
    attend(4)
    relay(1)
    attend(1)
    last(0)
    attend(2)
    last(1)
    for slot in (5, 6, 3, 7):
        if slot != 3:
            got(kbuf.at[slot], recv_p.at[0, slot - 4])
            got(vbuf.at[slot], recv_p.at[1, slot - 4])
        attend(slot)
    for n, buf in enumerate((kcb, vcb)):
        got(buf.at[2], recv_c.at[n, 0])
        sent.append(push(buf.at[2], buf.at[3], send_c.at[n, 2], recv_c.at[n, 2], (partner, ctx)))

    obuf[...] = (acc[...] / lrow[...]).astype(jnp.bfloat16)

    for d in range(8):
        j = (z + d) % 8
        piece = obuf.at[pl.ds(pl.multiple_of(j * ROWS, 16), ROWS), :]

        def remote():
            pltpu.make_async_remote_copy(
                src_ref=piece, dst_ref=ohome.at[z], send_sem=send_o.at[d], recv_sem=recv_o.at[0],
                device_id=(peer_view, peer_ctx + j), device_id_type=MESH,
            ).start()

        if d:
            remote()
        else:
            pl.when(jnp.logical_not(same))(remote)

            @pl.when(same)
            def _():
                pltpu.make_async_copy(piece, ohome.at[z], recv_o.at[0]).start()

    for copy in own:
        copy.wait()
    for n, buf in enumerate((kcb, vcb)):
        got(buf.at[1], recv_c.at[n, 1])
        got(buf.at[3], recv_c.at[n, 2])
    got(ohome, recv_o.at[0])

    for h in range(HEADS):
        cols = pl.ds(h * HEAD, HEAD)
        o_self = ohome[h].astype(jnp.float32)
        query = (qcb[:, cols].astype(jnp.float32) + o_self).astype(jnp.bfloat16).astype(jnp.float32)
        scores = [
            jnp.sum(query * kcb[b, :, cols].astype(jnp.float32), axis=1, keepdims=True) * SCALE
            for b in range(4)
        ]
        top = jnp.maximum(jnp.maximum(scores[0], scores[1]), jnp.maximum(scores[2], scores[3]))
        parts = [jnp.exp(s - top) for s in scores]
        total = (parts[0] + parts[1]) + (parts[2] + parts[3])
        mixed = 0.0
        for b in range(4):
            weight = (parts[b] / total).astype(jnp.bfloat16).astype(jnp.float32)
            mixed = mixed + weight * vcb[b, :, cols].astype(jnp.float32)
        o_cross = mixed.astype(jnp.bfloat16).astype(jnp.float32)
        out_ref[:, cols] = (o_self + o_cross).astype(jnp.bfloat16)

    for copy in sent:
        copy.wait_send()
    piece = k_in.at[:, pl.ds(0, HEAD)]
    for d in range(8):

        def drain():
            for n in range(3):
                pltpu.make_async_copy(piece, piece, send_a.at[n, d]).wait()
            pltpu.make_async_copy(piece, piece, send_o.at[d]).wait()

        if d:
            drain()
        else:
            pl.when(jnp.logical_not(same))(drain)


def body(*arrays):
    shape = arrays[0].shape
    flat = [a.reshape(ROWS, HEADS * HEAD) for a in arrays]
    b16, f32 = jnp.bfloat16, jnp.float32
    dma = pltpu.SemaphoreType.DMA
    out = pl.pallas_call(
        kernel,
        name="block",
        out_shape=jax.ShapeDtypeStruct((ROWS, HEADS * HEAD), b16),
        in_specs=[pl.BlockSpec(memory_space=pl.ANY)] * 6,
        out_specs=pl.BlockSpec(memory_space=pltpu.VMEM),
        scratch_shapes=[
            pltpu.VMEM((BLOCK, HEAD), b16),
            pltpu.VMEM((8, BLOCK, HEAD), b16),
            pltpu.VMEM((8, BLOCK, HEAD), b16),
            pltpu.VMEM((4, ROWS, HEADS * HEAD), b16),
            pltpu.VMEM((4, ROWS, HEADS * HEAD), b16),
            pltpu.VMEM((ROWS, HEADS * HEAD), b16),
            pltpu.VMEM((BLOCK, HEAD), b16),
            pltpu.VMEM((HEADS, ROWS, HEAD), b16),
            pltpu.VMEM((BLOCK, HEAD), f32),
            pltpu.VMEM((BLOCK, 1), f32),
            pltpu.VMEM((BLOCK, 1), f32),
            dma((3, 8)), dma((3,)),
            dma((2, 4)), dma((2, 4)),
            dma((2, 4)), dma((2, 4)),
            dma((2, 3)), dma((2, 3)),
            dma((8,)), dma((1,)),
            dma((3,)),
        ],
        compiler_params=pltpu.CompilerParams(collective_id=0, has_side_effects=True),
    )(*flat)
    return out.reshape(shape)


def solution(mesh):
    spec = P("view", "ctx", None)
    return jax.shard_map(body, mesh=mesh, in_specs=(spec,) * 6, out_specs=spec, check_vma=False)
```

time: 457 us -> 73.4 us (0.16)
  waiting for transfers between devices: 332 us -> 0 us
  Pallas kernels: 0 us -> 71.6 us
  local copies, waits for them, and re-layouts: 41.1 us -> 1.64 us
  matrix products: 32.9 us -> 0 us
  starting transfers between devices: 15.7 us -> 0 us
  between operations: 13.5 us -> 0.01 us
  other arithmetic: 12.8 us -> 0 us
  blocking collectives: 8.08 us -> 0 us
    all_gather x2 -> x0, waiting for transfers between devices: 322 us -> none  [the longest x1 180 us: body(): lax.all_gather(k_self, 'ctx', axis=1, tiled=True)]
    pallas_call x0 -> x1, Pallas kernels: none -> 71.6 us  [body(): pl.pallas_call(kernel, name='block', out_shape=jax.ShapeDtypeStruct((ROWS...]
    all_gather x2 -> x0, local copies, waits for them, and re-layouts: 36.8 us -> none  [the longest x1 18.4 us: body(): lax.all_gather(k_self, 'ctx', axis=1, tiled=True)]
    dot_general x3 -> x0, matrix products: 32.1 us -> none  [the longest x1 18.1 us: online_update(): jnp.einsum('ahqk,akhd->ahqd', weights_full.astype(jnp.bfloat16), value_ro...]
    all_to_all x3 -> x0, starting transfers between devices: 15.6 us -> none  [the longest x1 6.55 us: body(): lax.all_to_all(key_four, 'view', split_axis=1, concat_axis=0, tiled=True)]
    reduce_sum x1 -> x0, other arithmetic: 11 us -> none  [online_update(): running_sum = jnp.sum(weights_full, axis=-1)]
    all_to_all x1 -> x0, blocking collectives: 8.08 us -> none  [body(): lax.all_to_all(mixed_out, 'view', split_axis=0, concat_axis=1, tiled=True)]
    all_to_all x3 -> x0, waiting for transfers between devices: 7.82 us -> none  [the longest x1 3.96 us: body(): lax.all_to_all(merged, 'view', split_axis=1, concat_axis=0, tiled=True)]
  transfers between devices with their start and end apart: 5 -> 0, of which waited for: 4 -> 0; matrix products, arithmetic and copies ran while one was open for 19% -> 0% of each run, Pallas kernels for 0% -> 0%
where the time goes in v1:
time: 73.4 us; the launch traced here: 73.3 us
  Pallas kernels  71.6 us (98%)
  local copies, waits for them, and re-layouts  1.64 us (2%)
    pallas_call x1, Pallas kernels, body(): pl.pallas_call(kernel, name='block', out_shape=jax.ShapeDtypeStruct((ROWS...  71.6 us
    unnamed x1, local copies, waits for them, and re-layouts  1.64 us

profile of v1, /device:TPU:1, one launch (start us, length us, event | category | flops | bytes accessed | tf_op | source)
XLA Modules:
  0.0 73.3 jit_solution(4493644824500070556)
XLA Ops:
  0.0 71.6 %block.1 = bf16[112,1024]{1,0:T(8,128)(2,1)} custom-call(bf16[112,1024]{1,0:T(8,128)(2,1)} %bitcast.8, bf16[112,1024]{1,0:T(8,128)(2,1)} %bitcast.9, bf16[112,1024]{1,0:T(8,128)(2,1)} %bitcast.10, bf16[112,1024]{1,0:T(8,128)(2,1)} %bitcast.11, bf16[112,1024]{1,0:T(8,128)(2,1)} %bitcast.12, bf16[112,1024]{1,0:T(8,128)(2,1)} %bitcast.13), custom_call_target="tpu_custom_call" | custom-call | tf_op jit(solution)/shard_map/block/pallas_call | solution.py:246
  71.6 1.6 %copy.8 = bf16[1,112,1024]{2,1,0:T(8,128)(2,1)} copy(bf16[1,112,1024]{2,1,0:T(8,128)(2,1)} %bitcast.7) | data formatting | bytes 458752

commit v2 on v1

v2 whole, which is shorter than its diff:
```python
import math

import jax
import jax.numpy as jnp
from jax import lax
from jax.experimental import pallas as pl
from jax.experimental.pallas import tpu as pltpu
from jax.sharding import PartitionSpec as P

HEAD = 128
HEADS = 8
ROWS = 112
BLOCK = HEADS * ROWS
HALF = BLOCK // 2
SCALE = 1.0 / math.sqrt(HEAD)
SCALE2 = SCALE * math.log2(math.e)
MESH = pl.DeviceIdType.MESH
NT = (((1,), (1,)), ((), ()))

OWN, P_OWN, LEFT, RIGHT, P_LEFT, P_RIGHT, FAR, P_FAR = range(8)
PAIR = {OWN: P_OWN, LEFT: P_LEFT, RIGHT: P_RIGHT, FAR: P_FAR}
ORDER = (1, 7, 2, 6, 3, 5, 4, 0)
PLACE = {0: 0, 1: 1, 7: 2, 2: 3, 6: 4, 3: 5, 5: 6, 4: 7}


def kernel(
    q_in, k_in, v_in, qc_in, kc_in, vc_in, out_ref,
    qbuf, kbuf, vbuf, kcb, vcb, qcb, obuf, ohome, acc, mrow, lrow,
    send_a, recv_a, send_x, recv_x, send_p, recv_p, send_c, recv_c, send_o, recv_o, loc,
):
    view = lax.axis_index("view")
    ctx = lax.axis_index("ctx")
    ylo, core = view // 2, view % 2
    x, yhi, z = ctx // 16, (ctx // 8) % 2, ctx % 8
    rest = ctx % 16
    right = (view, ((x + 1) % 4) * 16 + rest)
    left = (view, ((x + 3) % 4) * 16 + rest)
    partner = (ylo * 2 + (1 - core), ctx)
    other = ((1 - ylo) * 2 + core, ctx)
    peer_view = ylo * 2 + yhi
    peer_ctx = x * 16 + core * 8
    same = core == yhi
    apart = core != yhi
    bufs = (kbuf, vbuf)

    barrier = pltpu.get_barrier_semaphore()
    for d in range(1, 8):
        pl.semaphore_signal(
            barrier, inc=1, device_id=(peer_view, peer_ctx + (z + d) % 8), device_id_type=MESH
        )

    @pl.when(apart)
    def _():
        pl.semaphore_signal(barrier, inc=1, device_id=(peer_view, peer_ctx + z), device_id_type=MESH)

    for dev in (right, left, partner, other):
        pl.semaphore_signal(barrier, inc=1, device_id=dev, device_id_type=MESH)
    pl.semaphore_wait(barrier, 11 + (core + yhi) % 2)

    def push(src, dst, send, recv, dev):
        pltpu.make_async_remote_copy(
            src_ref=src, dst_ref=dst, send_sem=send, recv_sem=recv, device_id=dev, device_id_type=MESH
        ).start()

    def got(buf, sem):
        pltpu.make_async_copy(buf, buf, sem).wait()

    def exchange(d, dev_z, src, dst, send, recv):
        def remote():
            push(src, dst, send, recv, (peer_view, peer_ctx + dev_z))

        if d:
            remote()
        else:
            pl.when(apart)(remote)

            @pl.when(same)
            def _():
                pltpu.make_async_copy(src, dst, recv).start()

    def spread(n, src, dst):
        for d in ORDER:
            h = (z + d) % 8
            exchange(
                d, h,
                src.at[:, pl.ds(pl.multiple_of(h * HEAD, HEAD), HEAD)],
                dst.at[pl.ds(PLACE[d] * ROWS, ROWS), :],
                send_a.at[n, d], recv_a.at[n, PLACE[d] // 4],
            )

    spread(0, k_in, kbuf.at[OWN])
    spread(2, q_in, qbuf)
    spread(1, v_in, vbuf.at[OWN])

    def part(n, slot, side):
        return bufs[n].at[slot, pl.ds(side * HALF, HALF), :]

    def share(n, slot, side):
        push(
            part(n, slot, side), part(n, PAIR[slot], side),
            send_p.at[n, slot, side], recv_p.at[n, slot, side], partner,
        )

    def own_half(n, side):
        got(part(n, OWN, side), recv_a.at[n, side])
        push(part(n, OWN, side), part(n, LEFT, side), send_x.at[n, 0, side], recv_x.at[n, LEFT, side], right)
        push(part(n, OWN, side), part(n, RIGHT, side), send_x.at[n, 1, side], recv_x.at[n, RIGHT, side], left)
        share(n, OWN, side)

    def relay(n, slot, side):
        got(part(n, slot, side), recv_x.at[n, slot, side])
        if (slot, side) == (LEFT, 0):
            push(part(n, LEFT, 0), part(n, FAR, 0), send_x.at[n, 2, 0], recv_x.at[n, FAR, 0], right)
        if (slot, side) == (RIGHT, 1):
            push(part(n, RIGHT, 1), part(n, FAR, 1), send_x.at[n, 2, 1], recv_x.at[n, FAR, 1], left)
        share(n, slot, side)

    def take(n, slot):
        for side in range(2):
            got(part(n, PAIR[slot], side), recv_p.at[n, slot, side])

    own_half(0, 0)
    own_half(0, 1)
    crossed = ((kc_in, kcb), (vc_in, vcb))
    for n, (src, buf) in enumerate(crossed):
        push(src, buf.at[2], send_c.at[n, 0], recv_c.at[n, 0], other)
        push(src, buf.at[1], send_c.at[n, 1], recv_c.at[n, 1], partner)
    own = [
        pltpu.make_async_copy(kc_in, kcb.at[0], loc.at[0]),
        pltpu.make_async_copy(vc_in, vcb.at[0], loc.at[1]),
        pltpu.make_async_copy(qc_in, qcb, loc.at[2]),
    ]
    for copy in own:
        copy.start()
    mrow[...] = jnp.full_like(mrow, -3e38)
    acc[...] = jnp.zeros_like(acc)
    lrow[...] = jnp.zeros_like(lrow)
    relay(0, LEFT, 0)
    relay(0, RIGHT, 0)
    relay(0, LEFT, 1)
    relay(0, RIGHT, 1)
    got(part(0, OWN, 0), recv_a.at[2, 0])
    got(part(0, OWN, 1), recv_a.at[2, 1])

    def top_step(i, carry):
        @pl.when(i == 1)
        def _():
            take(0, OWN)

        @pl.when(i == 3)
        def _():
            relay(0, FAR, 0)
            relay(0, FAR, 1)
            own_half(1, 0)

        @pl.when(i == 4)
        def _():
            take(0, LEFT)
            take(0, RIGHT)

        @pl.when(i == 6)
        def _():
            own_half(1, 1)

        @pl.when(i == 7)
        def _():
            take(0, FAR)

        scores = lax.dot_general(qbuf[...], kbuf[i], NT, preferred_element_type=jnp.float32)
        top = scores[:, :HEAD]
        for j in range(1, BLOCK // HEAD):
            top = jnp.maximum(top, scores[:, j * HEAD : (j + 1) * HEAD])
        mrow[...] = jnp.maximum(mrow[...], top)
        return carry

    lax.fori_loop(0, 8, top_step, 0)
    mrow[...] = jnp.broadcast_to(jnp.max(mrow[...], axis=1, keepdims=True), (BLOCK, HEAD)) * SCALE2

    def sum_step(i, carry):
        @pl.when(i == 1)
        def _():
            take(1, OWN)
            relay(1, LEFT, 0)
            relay(1, RIGHT, 0)

        @pl.when(i == 2)
        def _():
            relay(1, LEFT, 1)
            relay(1, RIGHT, 1)

        @pl.when(i == 4)
        def _():
            take(1, LEFT)
            take(1, RIGHT)
            for n, (_, buf) in enumerate(crossed):
                got(buf.at[2], recv_c.at[n, 0])
                push(buf.at[2], buf.at[3], send_c.at[n, 2], recv_c.at[n, 2], partner)

        @pl.when(i == 5)
        def _():
            relay(1, FAR, 0)
            relay(1, FAR, 1)

        @pl.when(i == 7)
        def _():
            take(1, FAR)

        scores = lax.dot_general(qbuf[...], kbuf[i], NT, preferred_element_type=jnp.float32)
        top = mrow[...]
        weights = [
            jnp.exp2(scores[:, j * HEAD : (j + 1) * HEAD] * SCALE2 - top) for j in range(BLOCK // HEAD)
        ]
        total = weights[0]
        for w in weights[1:]:
            total = total + w
        lrow[...] += total
        weights = jnp.concatenate([w.astype(jnp.bfloat16) for w in weights], axis=1)
        acc[...] += jnp.dot(weights, vbuf[i], preferred_element_type=jnp.float32)
        return carry

    lax.fori_loop(0, 8, sum_step, 0)
    obuf[...] = (acc[...] / jnp.sum(lrow[...], axis=1, keepdims=True)).astype(jnp.bfloat16)

    for d in ORDER:
        exchange(
            d, (z + 8 - d) % 8,
            obuf.at[pl.ds(PLACE[d] * ROWS, ROWS), :], ohome.at[z],
            send_o.at[d], recv_o.at[0],
        )

    for copy in own:
        copy.wait()
    for n, (_, buf) in enumerate(crossed):
        got(buf.at[1], recv_c.at[n, 1])
        got(buf.at[3], recv_c.at[n, 2])
    got(ohome, recv_o.at[0])

    for h in range(HEADS):
        cols = pl.ds(h * HEAD, HEAD)
        o_self = ohome[h].astype(jnp.float32)
        query = (qcb[:, cols].astype(jnp.float32) + o_self).astype(jnp.bfloat16).astype(jnp.float32)
        scores = [
            jnp.sum(query * kcb[b, :, cols].astype(jnp.float32), axis=1, keepdims=True) * SCALE
            for b in range(4)
        ]
        top = jnp.maximum(jnp.maximum(scores[0], scores[1]), jnp.maximum(scores[2], scores[3]))
        parts = [jnp.exp(s - top) for s in scores]
        total = (parts[0] + parts[1]) + (parts[2] + parts[3])
        mixed = 0.0
        for b in range(4):
            weight = (parts[b] / total).astype(jnp.bfloat16).astype(jnp.float32)
            mixed = mixed + weight * vcb[b, :, cols].astype(jnp.float32)
        o_cross = mixed.astype(jnp.bfloat16).astype(jnp.float32)
        out_ref[:, cols] = (o_self + o_cross).astype(jnp.bfloat16)

    for n in range(2):
        for side in range(2):
            piece = part(n, OWN, side)
            for k in range(3):
                got(piece, send_x.at[n, k, side])
            for slot in PAIR:
                got(piece, send_p.at[n, slot, side])
        for k in range(3):
            got(kcb.at[0], send_c.at[n, k])
    piece = qbuf.at[pl.ds(0, ROWS), :]
    for d in range(8):

        def drain():
            for n in range(3):
                got(piece, send_a.at[n, d])
            got(piece, send_o.at[d])

        if d:
            drain()
        else:
            pl.when(apart)(drain)


def body(*arrays):
    shape = arrays[0].shape
    flat = [a.reshape(ROWS, HEADS * HEAD) for a in arrays]
    b16, f32 = jnp.bfloat16, jnp.float32
    dma = pltpu.SemaphoreType.DMA
    out = pl.pallas_call(
        kernel,
        name="block",
        out_shape=jax.ShapeDtypeStruct((ROWS, HEADS * HEAD), b16),
        in_specs=[pl.BlockSpec(memory_space=pl.ANY)] * 6,
        out_specs=pl.BlockSpec(memory_space=pltpu.VMEM),
        scratch_shapes=[
            pltpu.VMEM((BLOCK, HEAD), b16),
            pltpu.VMEM((8, BLOCK, HEAD), b16),
            pltpu.VMEM((8, BLOCK, HEAD), b16),
            pltpu.VMEM((4, ROWS, HEADS * HEAD), b16),
            pltpu.VMEM((4, ROWS, HEADS * HEAD), b16),
            pltpu.VMEM((ROWS, HEADS * HEAD), b16),
            pltpu.VMEM((BLOCK, HEAD), b16),
            pltpu.VMEM((HEADS, ROWS, HEAD), b16),
            pltpu.VMEM((BLOCK, HEAD), f32),
            pltpu.VMEM((BLOCK, HEAD), f32),
            pltpu.VMEM((BLOCK, HEAD), f32),
            dma((3, 8)), dma((3, 2)),
            dma((2, 3, 2)), dma((2, 8, 2)),
            dma((2, 8, 2)), dma((2, 8, 2)),
            dma((2, 3)), dma((2, 3)),
            dma((8,)), dma((1,)),
            dma((3,)),
        ],
        compiler_params=pltpu.CompilerParams(collective_id=0, has_side_effects=True),
    )(*flat)
    return out.reshape(shape)


def solution(mesh):
    spec = P("view", "ctx", None)
    return jax.shard_map(body, mesh=mesh, in_specs=(spec,) * 6, out_specs=spec, check_vma=False)
```

time: 73.4 us -> 58.1 us (0.79)
  Pallas kernels: 71.6 us -> 56.3 us
    pallas_call x1, Pallas kernels: 71.6 us -> 56.3 us  [body(): pl.pallas_call(kernel, name='block', out_shape=jax.ShapeDtypeStruct((ROWS...]
where the time goes in v2:
time: 58.1 us; the launch traced here: 58 us
  Pallas kernels  56.3 us (97%)
  local copies, waits for them, and re-layouts  1.64 us (3%)
    pallas_call x1, Pallas kernels, body(): pl.pallas_call(kernel, name='block', out_shape=jax.ShapeDtypeStruct((ROWS...  56.3 us
    unnamed x1, local copies, waits for them, and re-layouts  1.64 us

profile of v2, /device:TPU:1, one launch (start us, length us, event | category | flops | bytes accessed | tf_op | source)
XLA Modules:
  0.0 58.0 jit_solution(12439562123254906922)
XLA Ops:
  0.0 56.3 %block.1 = bf16[112,1024]{1,0:T(8,128)(2,1)} custom-call(bf16[112,1024]{1,0:T(8,128)(2,1)} %bitcast.8, bf16[112,1024]{1,0:T(8,128)(2,1)} %bitcast.9, bf16[112,1024]{1,0:T(8,128)(2,1)} %bitcast.10, bf16[112,1024]{1,0:T(8,128)(2,1)} %bitcast.11, bf16[112,1024]{1,0:T(8,128)(2,1)} %bitcast.12, bf16[112,1024]{1,0:T(8,128)(2,1)} %bitcast.13), custom_call_target="tpu_custom_call" | custom-call | tf_op jit(solution)/shard_map/block/pallas_call | solution.py:284
  56.4 1.6 %copy.8 = bf16[1,112,1024]{2,1,0:T(8,128)(2,1)} copy(bf16[1,112,1024]{2,1,0:T(8,128)(2,1)} %bitcast.7) | data formatting | bytes 458752
